TPU v7x, 128 devices: a whole 4x4x4 slice. The times are simulated.
128 devices in a mesh: seq: 16 (over y, x), ctx: 8 (over z, core).
Axes of the slice: x: 4, y: 4, z: 4, core: 2. Of those that a mesh axis runs over, the one named last changes fastest.
Arguments:
- hidden_in: bfloat16 [16, 1024, 1024], P('seq', 'ctx'), may hold values from -6 to 6
- positions: int32 [16, 1024], P('seq', 'ctx'), may hold values from 0 to 1534, as said below
- starts: int32 [16, 2], P('seq'), may hold values from 0 to 768, as said below
- routes: int32 [16, 1024, 4], P('seq', 'ctx'), may hold values from 0 to 7, all different within a row; in each aligned block of 128 rows (0 to 127, 128 to 255, ..., all dimensions but the last counted through in order) at most 80 rows name the same one
- qkv_weight: bfloat16 [2048, 1024], P(('seq', 'ctx')), may hold values from -0.1875 to 0.1875
- out_weight: bfloat16 [1024, 1024], P(('seq', 'ctx')), may hold values from -1.5 to 1.5
- expert_in: bfloat16 [1024, 8, 1024], P(('seq', 'ctx')), may hold values from -0.1875 to 0.1875
- expert_out: bfloat16 [1024, 8, 512], P(('seq', 'ctx')), may hold values from -1.5 to 1.5
- router: bfloat16 [1024, 8], replicated, may hold values from -0.09375 to 0.09375
- attn_gain: bfloat16 [1024], replicated, may hold values from 0.25 to 1.75
- query_gain: bfloat16 [1024], replicated, may hold values from 0.25 to 1.75
- key_gain: bfloat16 [512], replicated, may hold values from 0.25 to 1.75
- mlp_gain: bfloat16 [1024], replicated, may hold values from 0.25 to 1.75
- out_grad: bfloat16 [16, 1024, 1024], P('seq', 'ctx'), may hold values from -6 to 6
Outputs:
- result: bfloat16 [16, 1024, 1024], P('seq', 'ctx')
- grad_input: float32 [16, 1024, 1024], P('seq', 'ctx')
- grad_qkv: float32 [2048, 1024], P(('seq', 'ctx'))
- grad_out: float32 [1024, 1024], P(('seq', 'ctx'))
- grad_expert_in: float32 [1024, 8, 1024], P(('seq', 'ctx'))
- grad_expert_out: float32 [1024, 8, 512], P(('seq', 'ctx'))
- grad_router: float32 [1024, 8], replicated
- grad_attn_gain: float32 [1024], replicated
- grad_query_gain: float32 [1024], replicated
- grad_key_gain: float32 [512], replicated
- grad_mlp_gain: float32 [1024], replicated
Inputs may be any that keep to these rules, and one draw needn't show every extreme that they name: `routes`: each row names 4 different experts; among the 128 tokens of one sequence on one device (aligned blocks), no expert is named by more than 80 of them. Piece k of a sequence starts at a token index from k * 512 to (k + 1) * 512 - 256; pieces never intersect. Within a sequence positions start at 0 and rise by 1 or 2 from token to token; the last token of every sequence has position 1534.
All inputs are finite; a program needn't handle non-finite values.
Results may differ from a plain program's by a relative error of at most 0.018.
Values may be sent and summed in bfloat16 or wider, within the bound.
A program may use at most 256 MiB of HBM per device.

v0:
```python
import jax
import jax.numpy as jnp
import numpy as np
from jax import lax
from jax.sharding import PartitionSpec as P

QUERY_HEADS = 16
KEY_VALUE_HEADS = 8
PIECE = 256
EPSILON = 1e-06
ROPE_BASE = 10000.0
MASKED = -1e30
F32 = jnp.float32
BF16 = jnp.bfloat16


def rms_scale(field):
    return lax.rsqrt(jnp.mean(field * field, axis=-1, keepdims=True) + EPSILON)


def rms_back(upstream, normed, scales):
    return scales * (upstream - normed * jnp.mean(upstream * normed, axis=-1, keepdims=True))


def rotary(field, cosine, sine):
    half = field.shape[-1] // 2
    a, b = (field[..., :half], field[..., half:])
    return jnp.concatenate([a * cosine - b * sine, b * cosine + a * sine], axis=-1)


def owner_of(s, c):
    if s < 8:
        return 8 * c + s
    if s < 12:
        return 64 + 4 * c + (s - 8)
    return 96 + 4 * c + (s - 12)


def dot(a, b, ca, cb):
    return lax.dot_general(a, b, (((ca,), (cb,)), ((), ())), preferred_element_type=F32)


def local(
    hidden_in,
    positions,
    starts,
    routes,
    qkv_weight,
    out_weight,
    expert_in,
    expert_out,
    router,
    attn_gain,
    query_gain,
    key_gain,
    mlp_gain,
    out_grad,
):
    rows = hidden_in.shape[1]
    width = hidden_in.shape[2]
    me = lax.axis_index("ctx")
    ns, nc = (lax.axis_size("seq"), lax.axis_size("ctx"))
    perm_in = [(owner_of(s, c), s * nc + c) for s in range(ns) for c in range(nc)]
    perm_out = [(b, a) for a, b in perm_in]
    ag = lambda v, ax: lax.all_gather(v, ax, axis=0, tiled=True)
    a2a = lambda v, sp, cc: lax.all_to_all(v, "ctx", sp, cc, tiled=True)
    w_qkv = ag(lax.ppermute(qkv_weight, ("seq", "ctx"), perm_in), "seq")
    w_out = ag(a2a(out_weight, 1, 0), "seq")
    w_in = ag(a2a(expert_in, 1, 0)[:, 0], "seq")
    w_down = ag(a2a(expert_out, 1, 0)[:, 0], "seq")
    x_own = hidden_in[0].astype(F32)
    x = ag(hidden_in[0], "ctx").astype(F32)
    dy = ag(out_grad[0], "ctx").astype(F32)
    pos = ag(positions[0], "ctx")
    routes_all = ag(routes[0], "ctx")
    s1 = rms_scale(x)
    attn_gain_f = attn_gain.astype(F32)
    x_low = (x * s1 * attn_gain_f).astype(BF16)
    qkv = dot(x_low, w_qkv, 1, 1)
    q, k, v = (qkv[:, :128], qkv[:, 128:192], qkv[:, 192:])
    sums = lax.psum(jnp.stack([jnp.sum(q * q, 1), jnp.sum(k * k, 1)]), "ctx")
    sq = lax.rsqrt(sums[0] / 1024 + EPSILON)[:, None]
    sk = lax.rsqrt(sums[1] / 512 + EPSILON)[:, None]
    nq, nk = (q * sq, k * sk)
    gq = lax.dynamic_slice(query_gain, (128 * me,), (128,)).astype(F32)
    gk = lax.dynamic_slice(key_gain, (64 * me,), (64,)).astype(F32)
    freq = ROPE_BASE ** (-jnp.arange(32, dtype=F32) * 2.0 / 64)
    ang = pos.astype(F32)[:, None] * freq
    cosv, sinv = (jnp.cos(ang), jnp.sin(ang))
    q_rot = rotary((nq * gq).reshape(-1, 2, 64), cosv[:, None], sinv[:, None]).astype(BF16)
    k_rot = rotary(nk * gk, cosv, sinv).astype(BF16)
    v_low = v.astype(BF16)
    places = jnp.arange(pos.shape[0], dtype=jnp.int32)
    inside = (places[:, None] >= starts) & (places[:, None] < starts + PIECE)
    label = jnp.sum(inside.astype(jnp.int32) * jnp.array([1, 2], jnp.int32), axis=1)
    allowed = (places[None, :] <= places[:, None]) | (label[:, None] == label[None, :]) & (
        label[:, None] > 0
    )
    scores = jnp.einsum("tgd,sd->gts", q_rot, k_rot, preferred_element_type=F32) * 0.125
    scores = jnp.where(allowed[None], scores, MASKED)
    p = jax.nn.softmax(scores, axis=-1)
    p_low = p.astype(BF16)
    attn = jnp.einsum("gts,sd->tgd", p_low, v_low, preferred_element_type=F32)
    attn_low = attn.reshape(-1, 128).astype(BF16)
    rs = lambda t: lax.psum_scatter(t, "ctx", scatter_dimension=0, tiled=True)
    mid = x_own + rs(dot(attn_low, w_out, 1, 1))
    s2 = rms_scale(mid)
    n2 = mid * s2
    gm = mlp_gain.astype(F32)
    h_own = (n2 * gm).astype(BF16)
    gates_own = jax.nn.softmax(jnp.dot(h_own, router, preferred_element_type=F32), axis=-1)
    h = ag(h_own, "ctx")
    gates = ag(gates_own, "ctx")
    routed = jnp.any(routes_all == me, axis=1)
    gate_c = jnp.where(routed, lax.dynamic_slice(gates, (0, me), (gates.shape[0], 1))[:, 0], 0.0)[
        :, None
    ]
    gu = dot(h, w_in, 1, 0)
    g, u = (gu[:, :512], gu[:, 512:])
    sig = jax.nn.sigmoid(g)
    sw = g * sig
    act = (sw * u).astype(BF16)
    res = dot(act, w_down, 1, 1)
    result = (mid + rs(gate_c * res)).astype(BF16)[None]
    d_res = (gate_c * dy).astype(BF16)
    d_gate_c = jnp.where(routed, jnp.sum(dy * res, axis=1), 0.0)
    d_act = dot(d_res, w_down, 1, 0)
    d_gu = jnp.concatenate([d_act * u * sig * (1.0 + g * (1.0 - sig)), d_act * sw], axis=1).astype(
        BF16
    )
    d_h = rs(dot(d_gu, w_in, 1, 1))
    g_in = dot(h, d_gu, 0, 0)
    g_down = dot(d_res, act, 0, 0)
    d_gates = a2a(d_gate_c[:, None], 0, 1)
    d_logits = (gates_own * (d_gates - jnp.sum(gates_own * d_gates, axis=1, keepdims=True))).astype(
        BF16
    )
    d_h = d_h + dot(d_logits, router, 1, 1)
    router_loc = dot(h_own, d_logits, 0, 0)
    mlp_loc = jnp.sum(d_h * n2, axis=0)
    d_mid = out_grad[0].astype(F32) + rms_back(d_h * gm, n2, s2)
    d_branch_own = d_mid.astype(BF16)
    d_branch = ag(d_branch_own, "ctx")
    d_attn = dot(d_branch, w_out, 1, 0).astype(BF16)
    g_out = dot(d_branch, attn_low, 0, 0)
    dp = jnp.einsum("tgd,sd->gts", d_attn.reshape(-1, 2, 64), v_low, preferred_element_type=F32)
    ds = (p * (dp - jnp.sum(p * dp, axis=-1, keepdims=True))).astype(BF16)
    dq = jnp.einsum("gts,sd->tgd", ds, k_rot, preferred_element_type=F32) * 0.125
    dk = jnp.einsum("gts,tgd->sd", ds, q_rot, preferred_element_type=F32) * 0.125
    dv = jnp.einsum("gts,tgd->sd", p_low, d_attn.reshape(-1, 2, 64), preferred_element_type=F32)
    dnq = rotary(dq, cosv[:, None], -sinv[:, None]).reshape(-1, 128)
    dnk = rotary(dk, cosv, -sinv)
    gq_loc = jnp.sum(dnq * nq, axis=0)
    gk_loc = jnp.sum(dnk * nk, axis=0)
    means = lax.psum(jnp.stack([jnp.sum(dnq * gq * nq, 1), jnp.sum(dnk * gk * nk, 1)]), "ctx")
    d_q = sq * (dnq * gq - nq * means[0][:, None] / 1024)
    d_k = sk * (dnk * gk - nk * means[1][:, None] / 512)
    d_qkv = jnp.concatenate([d_q, d_k, dv], axis=1).astype(BF16)
    d_x_low = rs(dot(d_qkv, w_qkv, 1, 0))
    g_qkv = dot(d_qkv, x_low, 0, 0)
    s1_own = rms_scale(x_own)
    n1_own = x_own * s1_own
    attn_loc = jnp.sum(d_x_low * n1_own, axis=0)
    grad_input = (d_mid + rms_back(d_x_low * attn_gain_f, n1_own, s1_own))[None]
    rss = lambda t: lax.psum_scatter(t, "seq", scatter_dimension=0, tiled=True)
    grad_qkv = lax.ppermute(rss(g_qkv), ("seq", "ctx"), perm_out)
    grad_out = a2a(rss(g_out), 0, 1)
    grad_in = a2a(rss(g_in)[:, None], 0, 1)
    grad_down = a2a(rss(g_down)[:, None], 0, 1)
    gq_all = lax.dynamic_update_slice(jnp.zeros((1024,), F32), gq_loc, (128 * me,))
    gk_all = lax.dynamic_update_slice(jnp.zeros((512,), F32), gk_loc, (64 * me,))
    ga, gqo, gko, gmo, gr = lax.psum(
        (attn_loc, gq_all, gk_all, mlp_loc, router_loc), ("seq", "ctx")
    )
    return (result, grad_input, grad_qkv, grad_out, grad_in, grad_down, gr, ga, gqo, gko, gmo)


def solution(mesh):
    t = ("seq", "ctx")
    in_specs = (
        P("seq", "ctx", None),
        P("seq", "ctx"),
        P("seq", None),
        P("seq", "ctx", None),
        P(t, None),
        P(t, None),
        P(t, None, None),
        P(t, None, None),
        P(),
        P(),
        P(),
        P(),
        P(),
        P("seq", "ctx", None),
    )
    out_specs = (
        P("seq", "ctx", None),
        P("seq", "ctx", None),
        P(t, None),
        P(t, None),
        P(t, None, None),
        P(t, None, None),
        P(),
        P(),
        P(),
        P(),
        P(),
    )
    return jax.shard_map(local, mesh=mesh, in_specs=in_specs, out_specs=out_specs, check_vma=False)
```

profile of v0, /device:TPU:1, one launch (start us, length us, event | category | flops | bytes accessed | tf_op | source)
XLA Modules:
  0.0 795.4 jit_solution(15250596640842094345)
XLA Ops:
  8.8 6.8 all-to-all-start
  15.6 3.1 collective-permute-start
  23.7 13.3 %all-gather.1 = s32[1,1024]{1,0:T(1,128)S(1)} all-gather(s32[1,128]{1,0:T(1,128)} %param.16), channel_id=3, replica_groups=mesh['seq'=16,'ctx'=8] {'ctx'}, dimensions={1}, use_global_device_ids=true | all-gather | bytes 4608 | tf_op jit(solution)/shard_map/all_gather | solution.py:65
  37.6 17.3 %all_gather.36 = bf16[1024,128]{1,0:T(8,128)(2,1)S(1)} all-gather(bf16[64,128]{1,0:T(8,128)(2,1)S(1)} %bitcast.193), channel_id=1, replica_groups=mesh['seq'=16,'ctx'=8] {'seq'}, dimensions={0}, use_global_device_ids=true | all-gather | bytes 278528 | tf_op jit(solution)/shard_map/all_gather | solution.py:65
  54.9 17.4 %all_gather.34 = bf16[256,1024]{1,0:T(8,128)(2,1)S(1)} all-gather(bf16[16,1024]{1,0:T(8,128)(2,1)S(1)} %collective-permute-done), channel_id=1, replica_groups=mesh['seq'=16,'ctx'=8] {'seq'}, dimensions={0}, use_global_device_ids=true | all-gather | bytes 557056 | tf_op jit(solution)/shard_map/all_gather | solution.py:65
  74.6 2.4 fusion.43
  77.2 22.6 %psum.49 = f32[2,1024]{1,0:T(2,128)S(1)} all-reduce(f32[2,1024]{1,0:T(2,128)S(1)} %pad_maximum_fusion.16), channel_id=1, replica_groups=mesh['seq'=16,'ctx'=8] {'ctx'}, use_global_device_ids=true, to_apply=%region_4.0 | all-reduce | flops 2048 | bytes 16384 | tf_op jit(solution)/shard_map/psum | solution.py:81
  102.1 5.4 fusion.97
  107.6 4.2 fusion.22
  111.9 2.7 fusion.99
  114.8 9.5 %all_to_all.120 = bf16[8,8,1024]{2,0,1:T(8,128)(2,1)} all-to-all(bf16[8,8,1024]{2,0,1:T(8,128)(2,1)S(1)} %copy.58), channel_id=1, replica_groups=mesh['seq'=16,'ctx'=8] {'ctx'}, dimensions={1} | all-to-all | bytes 262144 | tf_op jit(solution)/shard_map/all_to_all | solution.py:66
  124.5 22.8 %reduce-scatter.9.cloned.1.call-done = f32[128,1024]{1,0:T(8,128)} async-done(((f32[1024,1024]{1,0:T(8,128)}), f32[128,1024]{1,0:T(8,128)}) %reduce-scatter.9.cloned.1.call-update) | async-done | bytes 524304 | tf_op jit(solution)/shard_map/reduce_scatter | solution.py:105
  150.1 11.8 %all_to_all.121 = bf16[8,8,512]{2,0,1:T(8,128)(2,1)} all-to-all(bf16[8,8,512]{2,0,1:T(8,128)(2,1)S(1)} %copy.59), channel_id=1, replica_groups=mesh['seq'=16,'ctx'=8] {'ctx'}, dimensions={1} | all-to-all | bytes 131072 | tf_op jit(solution)/shard_map/all_to_all | solution.py:66
  162.7 12.3 %all-gather.2 = s32[1,1024,4]{1,2,0:T(4,128)S(1)} all-gather(s32[1,128,4]{1,2,0:T(4,128)S(1)} %copy-done.52), channel_id=4, replica_groups=mesh['seq'=16,'ctx'=8] {'ctx'}, dimensions={1}, use_global_device_ids=true | all-gather | bytes 18432 | tf_op jit(solution)/shard_map/all_gather | solution.py:65
  176.1 17.3 %all-gather.11.cloned.1.call-done = bf16[1024,1024]{1,0:T(8,128)(2,1)} async-done(((bf16[128,1024]{1,0:T(8,128)(2,1)}), bf16[1024,1024]{1,0:T(8,128)(2,1)}) %all-gather.11.cloned.1.call-update) | async-done | bytes 2097168 | tf_op jit(solution)/shard_map/all_gather | solution.py:65
  193.5 6.5 fusion.100
  200.0 2.8 multiply_convert_fusion.2
  202.8 33.4 %all-gather.15.cloned.1.call-done = bf16[1024,512]{1,0:T(8,128)(2,1)} async-done(((bf16[64,512]{1,0:T(8,128)(2,1)}), bf16[1024,512]{1,0:T(8,128)(2,1)}) %all-gather.15.cloned.1.call-update) | async-done | bytes 1048592 | tf_op jit(solution)/shard_map/all_gather | solution.py:65
  236.2 28.7 %all-gather.21.cloned.1.call-done = bf16[1,1024,1024]{2,1,0:T(8,128)(2,1)} async-done(((bf16[1,128,1024]{2,1,0:T(8,128)(2,1)}), bf16[1,1024,1024]{2,1,0:T(8,128)(2,1)}) %all-gather.21.cloned.1.call-update) | async-done | bytes 2097168 | tf_op jit(solution)/shard_map/all_gather | solution.py:65
  264.8 5.2 fusion.9
  270.7 3.5 all-to-all-start.3
  274.2 4.5 all-to-all-done.3
  278.7 13.3 %all_gather.38 = f32[1024,8]{0,1:T(8,128)S(1)} all-gather(f32[128,8]{0,1:T(8,128)S(1)} %get-tuple-element.25), channel_id=1, replica_groups=mesh['seq'=16,'ctx'=8] {'ctx'}, dimensions={0}, use_global_device_ids=true | all-gather | bytes 36864 | tf_op jit(solution)/shard_map/all_gather | solution.py:65
  292.0 5.4 multiply_convert_fusion.1
  298.8 4.3 fusion.20
  303.8 33.8 %reduce-scatter.13.cloned.1.call-done = f32[128,1024]{1,0:T(8,128)} async-done(((f32[1024,1024]{1,0:T(8,128)}), f32[128,1024]{1,0:T(8,128)}) %reduce-scatter.13.cloned.1.call-update) | async-done | bytes 524304 | tf_op jit(solution)/shard_map/reduce_scatter | solution.py:105
  341.8 4.5 fusion.34
  346.3 6.5 fusion.19
  352.9 16.5 %all-gather.17.cloned.1.call-done = bf16[1024,1024]{1,0:T(8,128)(2,1)} async-done(((bf16[128,1024]{1,0:T(8,128)(2,1)}), bf16[1024,1024]{1,0:T(8,128)(2,1)}) %all-gather.17.cloned.1.call-update) | async-done | bytes 2097168 | tf_op jit(solution)/shard_map/all_gather | solution.py:65
  369.3 2.4 convolution_convert_fusion
  371.8 4.8 fusion.1
  377.7 2.4 fusion.3
  384.6 12.2 %psum.50 = f32[2,1024]{1,0:T(2,128)S(1)} all-reduce(f32[2,1024]{1,0:T(2,128)S(1)} %pad_maximum_fusion.17), channel_id=1, replica_groups=mesh['seq'=16,'ctx'=8] {'ctx'}, use_global_device_ids=true, to_apply=%region_21.22 | all-reduce | flops 2048 | bytes 16384 | tf_op jit(solution)/shard_map/psum | solution.py:155
  398.4 5.0 fusion.29
  406.3 2.5 fusion.101
  408.9 3.9 fusion.55
  412.9 4.6 broadcast_multiply_fusion
  417.6 27.3 %reduce-scatter.23.cloned.1.call-done = f32[64,512]{1,0:T(8,128)} async-done(((f32[1024,512]{1,0:T(8,128)}), f32[64,512]{1,0:T(8,128)}) %reduce-scatter.23.cloned.1.call-update) | async-done | bytes 131088 | tf_op jit(solution)/shard_map/reduce_scatter | solution.py:165
  446.6 6.8 all-to-all-start.6
  453.3 72.0 %reduce-scatter.21.cloned.1.call-done = f32[64,1024]{1,0:T(8,128)} async-done(((f32[1024,1024]{1,0:T(8,128)}), f32[64,1024]{1,0:T(8,128)}) %reduce-scatter.21.cloned.1.call-update) | async-done | bytes 262160 | tf_op jit(solution)/shard_map/reduce_scatter | solution.py:165
  527.3 6.8 all-to-all-start.5
  534.1 66.5 %reduce-scatter.17.cloned.1.call-done = f32[16,1024]{1,0:T(8,128)} async-done(((f32[256,1024]{1,0:T(8,128)}), f32[16,1024]{1,0:T(8,128)}) %reduce-scatter.17.cloned.1.call-update) | async-done | bytes 65552 | tf_op jit(solution)/shard_map/reduce_scatter | solution.py:165
  600.6 5.0 collective-permute-start.1
  605.6 69.8 %reduce-scatter.19.cloned.1.call-done = f32[64,128]{1,0:T(8,128)} async-done(((f32[1024,128]{1,0:T(8,128)}), f32[64,128]{1,0:T(8,128)}) %reduce-scatter.19.cloned.1.call-update) | async-done | bytes 32784 | tf_op jit(solution)/shard_map/reduce_scatter | solution.py:165
  675.4 7.0 all-to-all-start.4
  684.6 2.6 all-to-all-done.4
  687.1 26.9 %reduce-scatter.15.cloned.1.call-done = f32[128,1024]{1,0:T(8,128)} async-done(((f32[1024,1024]{1,0:T(8,128)}), f32[128,1024]{1,0:T(8,128)}) %reduce-scatter.15.cloned.1.call-update) | async-done | bytes 524304 | tf_op jit(solution)/shard_map/reduce_scatter | solution.py:105
  715.4 68.8 %all-reduce = (f32[1024,8]{0,1:T(8,128)}, f32[1024]{0:T(1024)}, f32[1024]{0:T(1024)}, f32[512]{0:T(512)}, f32[1024]{0:T(1024)}) all-reduce(f32[1024,8]{0,1:T(8,128)S(1)} %fusion.102, f32[1024]{0:T(1024)S(1)} %get-tuple-element.17, f32[1024]{0:T(1024)S(1)} %dynamic_update_slice.6, ...), channel_id=1, replica_groups=mesh['seq'=16,'ctx'=8] {'seq','ctx'}, use_global_device_ids=true, to_apply=%region_28.29 | all-reduce | flops 11776 | bytes 94208 | tf_op jit(solution)/shard_map/psum | solution.py:172
  (223 shorter events, 43.4 us)
Async XLA Ops:
  8.0 167.0 %copy-start = (bf16[1024,8]{0,1:T(8,128)(2,1)S(1)}, bf16[1024,8]{0,1:T(8,128)(2,1)}, u32[]{:S(2)}) copy-start(bf16[1024,8]{0,1:T(8,128)(2,1)} %param.23) | copy-start | bytes 49156
  8.0 64.3 %all-gather.19.cloned.1.call-start = ((), (), s32[]{:S(2)}) async-start(), calls=%async_computation.27 | async-start | bytes 2359296 | tf_op jit(solution)/shard_map/all_gather | solution.py:65
  8.8 28.9 %all-to-all-start = ((bf16[8,8,128]{2,0,1:T(8,128)(2,1)}), bf16[8,8,128]{2,0,1:T(8,128)(2,1)S(1)}, u32[]{:S(2)}, u32[]{:S(2)}) async-start(bf16[8,8,128]{2,0,1:T(8,128)(2,1)} %bitcast.208), calls=%async_computation | async-start | bytes 32768 | tf_op jit(solution)/shard_map/all_to_all | solution.py:66
  15.6 131.7 %reduce-scatter.9.cloned.1.call-start = ((), (), s32[]{:S(2)}) async-start(), calls=%async_computation.15 | async-start | bytes 4718592 | tf_op jit(solution)/shard_map/reduce_scatter | solution.py:105
  15.6 39.3 %collective-permute-start = (bf16[16,1024]{1,0:T(8,128)(2,1)}, bf16[16,1024]{1,0:T(8,128)(2,1)S(1)}, u32[]{:S(2)}, u32[]{:S(2)}) collective-permute-start(bf16[16,1024]{1,0:T(8,128)(2,1)} %param.19), channel_id=1, source_target_pairs={{0,0},{8,1},{16,2},{24,3},{32,4},{40,5},{48,6},{56,7},{1,8},{9,9},... | collective-permute-start | bytes 98312 | tf_op jit(solution)/shard_map/ppermute | solution.py:67
  20.0 80.0 %copy-start.43 = (f32[128]{0:T(128)}, f32[128]{0:T(128)S(1)}, u32[]{:S(2)}) copy-start(f32[128]{0:T(128)S(1)} %dynamic-slice_convert_fusion) | copy-start | bytes 1540
  23.1 76.8 %copy-start.45 = (f32[64]{0:T(128)}, f32[64]{0:T(128)S(1)}, u32[]{:S(2)}) copy-start(f32[64]{0:T(128)S(1)} %dynamic-slice_convert_fusion.1) | copy-start | bytes 772
  23.7 53.3 %copy-start.31 = (f32[1024]{0:T(1024)}, f32[1024]{0:T(1024)S(1)}, u32[]{:S(2)}) copy-start(f32[1024]{0:T(1024)S(1)} %convert_element_type.74) | copy-start | bytes 12292
  54.9 57.0 %copy-start.5 = (bf16[1024,128]{1,0:T(8,128)(2,1)}, bf16[1024,128]{1,0:T(8,128)(2,1)S(1)}, u32[]{:S(2)}) copy-start(bf16[1024,128]{1,0:T(8,128)(2,1)S(1)} %all_gather.36) | copy-start | bytes 786436
  99.9 7.7 copy-start.26
  99.9 7.7 copy-start.28
  111.9 12.6 %copy-start.51 = (bf16[1024]{0:T(1024)(128)(2,1)S(1)}, bf16[1024]{0:T(1024)(128)(2,1)}, u32[]{:S(2)}) copy-start(bf16[1024]{0:T(1024)(128)(2,1)} %param.27) | copy-start | bytes 6148
  111.9 35.4 %copy-start.3 = (bf16[1,128,1024]{2,1,0:T(8,128)(2,1)S(1)}, bf16[1,128,1024]{2,1,0:T(8,128)(2,1)}, u32[]{:S(2)}) copy-start(bf16[1,128,1024]{2,1,0:T(8,128)(2,1)} %param.15) | copy-start | bytes 786436
  114.7 35.4 %copy-start.30 = (bf16[8,8,512]{2,1,0:T(8,128)(2,1)S(1)}, bf16[8,8,512]{2,1,0:T(8,128)(2,1)}, u32[]{:S(2)}) copy-start(bf16[8,8,512]{2,1,0:T(8,128)(2,1)} %param.22) | copy-start | bytes 196612
  114.7 48.0 %copy-start.52 = (s32[1,128,4]{1,2,0:T(4,128)S(1)}, s32[1,128,4]{1,2,0:T(4,128)}, u32[]{:S(2)}) copy-start(s32[1,128,4]{1,2,0:T(4,128)} %param.18) | copy-start | bytes 6148
  114.7 61.4 %all-gather.13.cloned.1.call-start = ((), (), s32[]{:S(2)}) async-start(), calls=%async_computation.17 | async-start | bytes 2228224 | tf_op jit(solution)/shard_map/all_gather | solution.py:65
  124.4 69.0 %all-gather.11.cloned.1.call-start = ((), (), s32[]{:S(2)}) async-start(), calls=%async_computation.16 | async-start | bytes 2359296 | tf_op jit(solution)/shard_map/all_gather | solution.py:65
  124.5 25.5 %copy-start.24 = (f32[1024]{0:T(1024)}, f32[1024]{0:T(1024)S(1)}, u32[]{:S(2)}) copy-start(f32[1024]{0:T(1024)S(1)} %convert_element_type.83) | copy-start | bytes 12292
  150.0 86.2 %all-gather.15.cloned.1.call-start = ((), (), s32[]{:S(2)}) async-start(), calls=%async_computation.18 | async-start | bytes 1114112 | tf_op jit(solution)/shard_map/all_gather | solution.py:65
  161.9 102.9 %all-gather.21.cloned.1.call-start = ((), (), s32[]{:S(2)}) async-start(), calls=%async_computation.28 | async-start | bytes 2359296 | tf_op jit(solution)/shard_map/all_gather | solution.py:65
  270.7 8.0 %all-to-all-start.3 = ((f32[8,128,1]{1,2,0:T(1,128)}), f32[8,128,1]{1,2,0:T(1,128)S(1)}, u32[]{:S(2)}, u32[]{:S(2)}) async-start(f32[8,128,1]{1,2,0:T(1,128)} %bitcast.30), calls=%async_computation.6 | async-start | bytes 8192 | tf_op jit(solution)/shard_map/all_to_all | solution.py:66
  274.1 63.5 %reduce-scatter.13.cloned.1.call-start = ((), (), s32[]{:S(2)}) async-start(), calls=%async_computation.20 | async-start | bytes 4718592 | tf_op jit(solution)/shard_map/reduce_scatter | solution.py:105
  292.0 6.8 copy-start.57
  303.2 66.2 %all-gather.17.cloned.1.call-start = ((), (), s32[]{:S(2)}) async-start(), calls=%async_computation.21 | async-start | bytes 2359296 | tf_op jit(solution)/shard_map/all_gather | solution.py:65
  341.6 103.3 %reduce-scatter.23.cloned.1.call-start = ((), (), s32[]{:S(2)}) async-start(), calls=%async_computation.26 | async-start | bytes 2228224 | tf_op jit(solution)/shard_map/reduce_scatter | solution.py:165
  346.3 179.1 %reduce-scatter.21.cloned.1.call-start = ((), (), s32[]{:S(2)}) async-start(), calls=%async_computation.25 | async-start | bytes 4456448 | tf_op jit(solution)/shard_map/reduce_scatter | solution.py:165
  352.8 16.5 %copy-start.6 = (bf16[1024,128]{1,0:T(8,128)(2,1)S(1)}, bf16[1024,128]{1,0:T(8,128)(2,1)}, u32[]{:S(2)}) copy-start(bf16[1024,128]{1,0:T(8,128)(2,1)} %copy-done.5) | copy-start | bytes 786436
  352.8 19.0 %copy-start.40 = (f32[2,1024]{1,0:T(2,128)S(1)}, f32[2,1024]{1,0:T(2,128)}, u32[]{:S(2)}) copy-start(f32[2,1024]{1,0:T(2,128)} %copy-done.39) | copy-start | bytes 24580
  352.8 247.7 %reduce-scatter.17.cloned.1.call-start = ((), (), s32[]{:S(2)}) async-start(), calls=%async_computation.23 | async-start | bytes 1114112 | tf_op jit(solution)/shard_map/reduce_scatter | solution.py:165
  406.0 269.4 %reduce-scatter.19.cloned.1.call-start = ((), (), s32[]{:S(2)}) async-start(), calls=%async_computation.24 | async-start | bytes 557056 | tf_op jit(solution)/shard_map/reduce_scatter | solution.py:165
  408.9 305.2 %reduce-scatter.15.cloned.1.call-start = ((), (), s32[]{:S(2)}) async-start(), calls=%async_computation.22 | async-start | bytes 4718592 | tf_op jit(solution)/shard_map/reduce_scatter | solution.py:105
  412.9 371.4 %reduce-scatter.11.cloned.1.call-start = ((), (), s32[]{:S(2)}) async-start(), calls=%async_computation.19 | async-start | bytes 4718592 | tf_op jit(solution)/shard_map/reduce_scatter | solution.py:105
  417.5 116.6 %copy-start.55 = (f32[128]{0:T(128)S(1)}, f32[128]{0:T(128)}, u32[]{:S(2)}) copy-start(f32[128]{0:T(128)} %get-tuple-element.40) | copy-start | bytes 1540
  417.5 264.9 %copy-start.4 = (bf16[128,1024]{1,0:T(8,128)(2,1)S(1)}, bf16[128,1024]{1,0:T(8,128)(2,1)}, u32[]{:S(2)}) copy-start(bf16[128,1024]{1,0:T(8,128)(2,1)} %multiply_convert_fusion.4) | copy-start | bytes 786436
  417.5 264.9 %copy-start.35 = (bf16[128,8]{0,1:T(8,128)(2,1)S(1)}, bf16[128,8]{0,1:T(8,128)(2,1)}, u32[]{:S(2)}) copy-start(bf16[128,8]{0,1:T(8,128)(2,1)} %multiply_convert_fusion.6) | copy-start | bytes 6148
  417.5 266.7 %copy-start.54 = (f32[128]{0:T(128)S(1)}, f32[128]{0:T(128)}, u32[]{:S(2)}) copy-start(f32[128]{0:T(128)} %get-tuple-element.11) | copy-start | bytes 1540
  417.5 266.8 %copy-start.56 = (f32[64]{0:T(128)S(1)}, f32[64]{0:T(128)}, u32[]{:S(2)}) copy-start(f32[64]{0:T(128)} %get-tuple-element.13) | copy-start | bytes 772
  417.5 296.6 %copy-start.33 = (f32[1024]{0:T(1024)S(1)}, f32[1024]{0:T(1024)}, u32[]{:S(2)}) copy-start(f32[1024]{0:T(1024)} %copy-done.31) | copy-start | bytes 12292
  417.5 297.9 %copy-start.36 = (f32[1024]{0:T(1024)S(1)}, f32[1024]{0:T(1024)}, u32[]{:S(2)}) copy-start(f32[1024]{0:T(1024)} %get-tuple-element.15) | copy-start | bytes 12292
  417.6 366.7 %copy-start.7 = (bf16[1,128,1024]{2,1,0:T(8,128)(2,1)S(1)}, bf16[1,128,1024]{2,1,0:T(8,128)(2,1)}, u32[]{:S(2)}) copy-start(bf16[1,128,1024]{2,1,0:T(8,128)(2,1)} %param.28) | copy-start | bytes 786436
  417.6 366.7 %copy-start.25 = (f32[1024]{0:T(1024)S(1)}, f32[1024]{0:T(1024)}, u32[]{:S(2)}) copy-start(f32[1024]{0:T(1024)} %copy-done.24) | copy-start | bytes 12292
  417.6 366.7 %copy-start.42 = (f32[128]{0:T(128)S(1)}, f32[128]{0:T(128)}, u32[]{:S(2)}) copy-start(f32[128]{0:T(128)} %copy-done.41) | copy-start | bytes 1540
  417.6 366.7 %copy-start.50 = (f32[128]{0:T(128)S(1)}, f32[128]{0:T(128)}, u32[]{:S(2)}) copy-start(f32[128]{0:T(128)} %copy-done.49) | copy-start | bytes 1540
  417.6 370.2 %copy-start.1 = (bf16[1024,8]{0,1:T(8,128)(2,1)S(1)}, bf16[1024,8]{0,1:T(8,128)(2,1)}, u32[]{:S(2)}) copy-start(bf16[1024,8]{0,1:T(8,128)(2,1)} %param.23) | copy-start | bytes 49156
  446.6 80.7 %all-to-all-start.6 = ((f32[64,1,512]{2,1,0:T(1,128)}), f32[64,1,512]{2,1,0:T(1,128)S(1)}, u32[]{:S(2)}, u32[]{:S(2)}) async-start(f32[64,1,512]{2,1,0:T(1,128)} %copy.68), calls=%async_computation.14 | async-start | bytes 262144 | tf_op jit(solution)/shard_map/all_to_all | solution.py:66
  527.3 78.3 %all-to-all-start.5 = ((f32[64,1,1024]{2,1,0:T(1,128)}), f32[64,1,1024]{2,1,0:T(1,128)S(1)}, u32[]{:S(2)}, u32[]{:S(2)}) async-start(f32[64,1,1024]{2,1,0:T(1,128)} %copy.66), calls=%async_computation.12 | async-start | bytes 524288 | tf_op jit(solution)/shard_map/all_to_all | solution.py:66
  600.6 86.6 %collective-permute-start.1 = (f32[16,1024]{1,0:T(8,128)}, f32[16,1024]{1,0:T(8,128)S(1)}, u32[]{:S(2)}, u32[]{:S(2)}) collective-permute-start(f32[16,1024]{1,0:T(8,128)} %reduce-scatter.17.cloned.1.call-done), channel_id=1, source_target_pairs={{0,0},{1,8},{2,16},{3,24},{4,32},{5,40},{6,48},{7,56},{8,1},{9,9},... | collective-permute-start | bytes 196616 | tf_op jit(solution)/shard_map/ppermute | solution.py:166
  675.4 11.7 %all-to-all-start.4 = ((f32[8,8,128]{2,1,0:T(8,128)}), f32[8,8,128]{2,1,0:T(8,128)S(1)}, u32[]{:S(2)}, u32[]{:S(2)}) async-start(f32[8,8,128]{2,1,0:T(8,128)} %bitcast.198), calls=%async_computation.10 | async-start | bytes 65536 | tf_op jit(solution)/shard_map/all_to_all | solution.py:66
  (35 other events, 120.6 us)
Sparse Core Ops, SparseCore 0:
  10.6 28.9 all-gather.18
  114.8 32.4 reduce-scatter.8
  303.3 34.2 reduce-scatter.12
Sparse Core Ops, SparseCore 1:
  124.5 39.9 all-gather.12
  166.6 26.8 all-gather.10
  195.5 40.6 all-gather.14
  237.9 26.9 all-gather.20
  341.6 27.7 all-gather.16
  372.6 72.2 reduce-scatter.22
  448.5 76.8 reduce-scatter.20
  528.4 72.1 reduce-scatter.16
  603.9 71.4 reduce-scatter.18
  677.8 36.2 reduce-scatter.14
  716.4 37.5 reduce-scatter.10
where the time goes:
time: 803 us; the launch traced here: 795 us
  waiting for transfers between devices  424 us (53%)
  blocking collectives  199 us (25%)
  matrix products  73.4 us (9%)
  starting transfers between devices  39.8 us (5%)
  other arithmetic  32.9 us (4%)
  between operations  16.8 us (2%)
  local copies, waits for them, and re-layouts  10.3 us (1%)
    reduce_scatter x4, waiting for transfers between devices, local(): rss = lambda t: lax.psum_scatter(t, 'seq', scatter_dimension=0, tiled=True)  236 us
    all_gather x6, waiting for transfers between devices, local(): ag = lambda v, ax: lax.all_gather(v, ax, axis=0, tiled=True)  95.8 us
    reduce_scatter x4, waiting for transfers between devices, local(): rs = lambda t: lax.psum_scatter(t, 'ctx', scatter_dimension=0, tiled=True)  83.6 us
    all_gather x5, blocking collectives, local(): ag = lambda v, ax: lax.all_gather(v, ax, axis=0, tiled=True)  73.5 us
    psum x1, blocking collectives, local(): lax.psum((attn_loc, gq_all, gk_all, mlp_loc, router_loc), ('seq', 'ctx'))  68.8 us
    dot_general x14, matrix products, dot(): lax.dot_general(a, b, (((ca,), (cb,)), ((), ())), preferred_element_type=...  50.5 us
    all_to_all x5, starting transfers between devices, local(): a2a = lambda v, sp, cc: lax.all_to_all(v, 'ctx', sp, cc, tiled=True)  30.9 us
    psum x1, blocking collectives, local(): sums = lax.psum(jnp.stack([jnp.sum(q * q, 1), jnp.sum(k * k, 1)]), 'ctx')  22.6 us
  transfers between devices with their start and end apart: 21, of which 13 were waited for; matrix products, arithmetic and copies ran while one was open for 9% of the time, Pallas kernels for 0%

commit v1 on v0

--- a/solution.py
+++ b/solution.py
@@ -78,7 +78,7 @@
     x_low = (x * s1 * attn_gain_f).astype(BF16)
     qkv = dot(x_low, w_qkv, 1, 1)
     q, k, v = (qkv[:, :128], qkv[:, 128:192], qkv[:, 192:])
-    sums = lax.psum(jnp.stack([jnp.sum(q * q, 1), jnp.sum(k * k, 1)]), "ctx")
+    sums = jnp.sum(lax.all_gather(jnp.stack([jnp.sum(q * q, 1), jnp.sum(k * k, 1)]), "ctx"), axis=0)
     sq = lax.rsqrt(sums[0] / 1024 + EPSILON)[:, None]
     sk = lax.rsqrt(sums[1] / 512 + EPSILON)[:, None]
     nq, nk = (q * sq, k * sk)

time: 803 us -> 802 us (level)
    all_gather x0 -> x1, blocking collectives: none -> 23.2 us  [local(): lax.all_gather(jnp.stack([jnp.sum(q * q, 1), jnp.sum(k * k, 1)]), 'ctx')]
    psum x1 -> x0, blocking collectives: 22.6 us -> none  [local(): sums = lax.psum(jnp.stack([jnp.sum(q * q, 1), jnp.sum(k * k, 1)]), 'ctx')]
where the time goes in v1:
time: 802 us; the launch traced here: 794 us
  waiting for transfers between devices  424 us (53%)
  blocking collectives  198 us (25%)
  matrix products  73.5 us (9%)
  starting transfers between devices  39.9 us (5%)
  other arithmetic  31.1 us (4%)
  between operations  16.8 us (2%)
  local copies, waits for them, and re-layouts  10.7 us (1%)
    reduce_scatter x4, waiting for transfers between devices, local(): rss = lambda t: lax.psum_scatter(t, 'seq', scatter_dimension=0, tiled=True)  236 us
    all_gather x6, waiting for transfers between devices, local(): ag = lambda v, ax: lax.all_gather(v, ax, axis=0, tiled=True)  95.8 us
    reduce_scatter x4, waiting for transfers between devices, local(): rs = lambda t: lax.psum_scatter(t, 'ctx', scatter_dimension=0, tiled=True)  84.2 us
    all_gather x5, blocking collectives, local(): ag = lambda v, ax: lax.all_gather(v, ax, axis=0, tiled=True)  73.5 us
    psum x1, blocking collectives, local(): lax.psum((attn_loc, gq_all, gk_all, mlp_loc, router_loc), ('seq', 'ctx'))  68.7 us
    dot_general x14, matrix products, dot(): lax.dot_general(a, b, (((ca,), (cb,)), ((), ())), preferred_element_type=...  50.6 us
    all_to_all x5, starting transfers between devices, local(): a2a = lambda v, sp, cc: lax.all_to_all(v, 'ctx', sp, cc, tiled=True)  30.9 us
    all_gather x1, blocking collectives, local(): lax.all_gather(jnp.stack([jnp.sum(q * q, 1), jnp.sum(k * k, 1)]), 'ctx')  23.2 us
  transfers between devices with their start and end apart: 21, of which 13 were waited for; matrix products, arithmetic and copies ran while one was open for 9% of the time, Pallas kernels for 0%

profile of v1, /device:TPU:1, one launch (start us, length us, event | category | flops | bytes accessed | tf_op | source)
XLA Modules:
  0.0 794.2 jit_solution(3438188153228695705)
XLA Ops:
  8.8 6.8 all-to-all-start
  15.6 3.1 collective-permute-start
  23.2 13.3 %all-gather.2 = s32[1,1024]{1,0:T(1,128)S(1)} all-gather(s32[1,128]{1,0:T(1,128)} %param.16), channel_id=4, replica_groups=mesh['seq'=16,'ctx'=8] {'ctx'}, dimensions={1}, use_global_device_ids=true | all-gather | bytes 4608 | tf_op jit(solution)/shard_map/all_gather | solution.py:65
  36.5 17.2 %all_gather.44 = bf16[1024,128]{1,0:T(8,128)(2,1)S(1)} all-gather(bf16[64,128]{1,0:T(8,128)(2,1)S(1)} %bitcast.195), channel_id=1, replica_groups=mesh['seq'=16,'ctx'=8] {'seq'}, dimensions={0}, use_global_device_ids=true | all-gather | bytes 278528 | tf_op jit(solution)/shard_map/all_gather | solution.py:65
  53.8 17.4 %all_gather.40 = bf16[256,1024]{1,0:T(8,128)(2,1)S(1)} all-gather(bf16[16,1024]{1,0:T(8,128)(2,1)S(1)} %collective-permute-done), channel_id=1, replica_groups=mesh['seq'=16,'ctx'=8] {'seq'}, dimensions={0}, use_global_device_ids=true | all-gather | bytes 557056 | tf_op jit(solution)/shard_map/all_gather | solution.py:65
  73.5 2.4 fusion.43
  76.1 23.2 %all-gather.5 = f32[8,2,1024]{2,1,0:T(2,128)S(1)} all-gather(f32[1,2,1024]{2,1,0:T(2,128)S(1)} %maximum_bitcast_fusion.6), channel_id=3, replica_groups=mesh['seq'=16,'ctx'=8] {'ctx'}, dimensions={0}, use_global_device_ids=true | all-gather | bytes 73728 | tf_op jit(solution)/shard_map/all_gather | solution.py:81
  101.2 5.5 fusion.97
  106.8 4.2 fusion.22
  111.1 2.8 fusion.99
  114.0 8.5 %all_to_all.120 = bf16[8,8,1024]{2,0,1:T(8,128)(2,1)} all-to-all(bf16[8,8,1024]{2,0,1:T(8,128)(2,1)S(1)} %copy.58), channel_id=1, replica_groups=mesh['seq'=16,'ctx'=8] {'ctx'}, dimensions={1} | all-to-all | bytes 262144 | tf_op jit(solution)/shard_map/all_to_all | solution.py:66
  122.6 23.4 %reduce-scatter.9.cloned.1.call-done = f32[128,1024]{1,0:T(8,128)} async-done(((f32[1024,1024]{1,0:T(8,128)}), f32[128,1024]{1,0:T(8,128)}) %reduce-scatter.9.cloned.1.call-update) | async-done | bytes 524304 | tf_op jit(solution)/shard_map/reduce_scatter | solution.py:105
  148.8 11.8 %all_to_all.121 = bf16[8,8,512]{2,0,1:T(8,128)(2,1)} all-to-all(bf16[8,8,512]{2,0,1:T(8,128)(2,1)S(1)} %copy.59), channel_id=1, replica_groups=mesh['seq'=16,'ctx'=8] {'ctx'}, dimensions={1} | all-to-all | bytes 131072 | tf_op jit(solution)/shard_map/all_to_all | solution.py:66
  161.3 12.3 %all-gather.3 = s32[1,1024,4]{1,2,0:T(4,128)S(1)} all-gather(s32[1,128,4]{1,2,0:T(4,128)S(1)} %copy-done.53), channel_id=5, replica_groups=mesh['seq'=16,'ctx'=8] {'ctx'}, dimensions={1}, use_global_device_ids=true | all-gather | bytes 18432 | tf_op jit(solution)/shard_map/all_gather | solution.py:65
  174.8 17.4 %all-gather.13.cloned.1.call-done = bf16[1024,1024]{1,0:T(8,128)(2,1)} async-done(((bf16[128,1024]{1,0:T(8,128)(2,1)}), bf16[1024,1024]{1,0:T(8,128)(2,1)}) %all-gather.13.cloned.1.call-update) | async-done | bytes 2097168 | tf_op jit(solution)/shard_map/all_gather | solution.py:65
  192.1 6.5 fusion.100
  198.7 2.8 multiply_convert_fusion.2
  201.5 33.3 %all-gather.17.cloned.1.call-done = bf16[1024,512]{1,0:T(8,128)(2,1)} async-done(((bf16[64,512]{1,0:T(8,128)(2,1)}), bf16[1024,512]{1,0:T(8,128)(2,1)}) %all-gather.17.cloned.1.call-update) | async-done | bytes 1048592 | tf_op jit(solution)/shard_map/all_gather | solution.py:65
  234.9 28.7 %all-gather.23.cloned.1.call-done = bf16[1,1024,1024]{2,1,0:T(8,128)(2,1)} async-done(((bf16[1,128,1024]{2,1,0:T(8,128)(2,1)}), bf16[1,1024,1024]{2,1,0:T(8,128)(2,1)}) %all-gather.23.cloned.1.call-update) | async-done | bytes 2097168 | tf_op jit(solution)/shard_map/all_gather | solution.py:65
  263.5 5.2 fusion.9
  269.4 3.5 all-to-all-start.3
  272.9 4.5 all-to-all-done.3
  277.4 13.3 %all_gather.46 = f32[1024,8]{0,1:T(8,128)S(1)} all-gather(f32[128,8]{0,1:T(8,128)S(1)} %get-tuple-element.25), channel_id=1, replica_groups=mesh['seq'=16,'ctx'=8] {'ctx'}, dimensions={0}, use_global_device_ids=true | all-gather | bytes 36864 | tf_op jit(solution)/shard_map/all_gather | solution.py:65
  290.7 5.4 multiply_convert_fusion.1
  297.5 4.3 fusion.20
  302.5 33.9 %reduce-scatter.13.cloned.1.call-done = f32[128,1024]{1,0:T(8,128)} async-done(((f32[1024,1024]{1,0:T(8,128)}), f32[128,1024]{1,0:T(8,128)}) %reduce-scatter.13.cloned.1.call-update) | async-done | bytes 524304 | tf_op jit(solution)/shard_map/reduce_scatter | solution.py:105
  340.6 4.5 fusion.34
  345.1 6.5 fusion.19
  351.7 16.4 %all-gather.19.cloned.1.call-done = bf16[1024,1024]{1,0:T(8,128)(2,1)} async-done(((bf16[128,1024]{1,0:T(8,128)(2,1)}), bf16[1024,1024]{1,0:T(8,128)(2,1)}) %all-gather.19.cloned.1.call-update) | async-done | bytes 2097168 | tf_op jit(solution)/shard_map/all_gather | solution.py:65
  368.1 2.4 convolution_convert_fusion
  370.6 4.8 fusion.1
  376.5 2.4 fusion.3
  383.4 12.2 %psum.42 = f32[2,1024]{1,0:T(2,128)S(1)} all-reduce(f32[2,1024]{1,0:T(2,128)S(1)} %pad_maximum_fusion.16), channel_id=1, replica_groups=mesh['seq'=16,'ctx'=8] {'ctx'}, use_global_device_ids=true, to_apply=%region_21.22 | all-reduce | flops 2048 | bytes 16384 | tf_op jit(solution)/shard_map/psum | solution.py:155
  397.2 5.0 fusion.29
  405.1 2.5 fusion.101
  407.7 3.9 fusion.55
  411.7 4.6 broadcast_multiply_fusion
  416.4 27.3 %reduce-scatter.23.cloned.1.call-done = f32[64,512]{1,0:T(8,128)} async-done(((f32[1024,512]{1,0:T(8,128)}), f32[64,512]{1,0:T(8,128)}) %reduce-scatter.23.cloned.1.call-update) | async-done | bytes 131088 | tf_op jit(solution)/shard_map/reduce_scatter | solution.py:165
  445.4 6.7 all-to-all-start.6
  452.2 72.1 %reduce-scatter.21.cloned.1.call-done = f32[64,1024]{1,0:T(8,128)} async-done(((f32[1024,1024]{1,0:T(8,128)}), f32[64,1024]{1,0:T(8,128)}) %reduce-scatter.21.cloned.1.call-update) | async-done | bytes 262160 | tf_op jit(solution)/shard_map/reduce_scatter | solution.py:165
  526.2 6.8 all-to-all-start.5
  533.0 66.5 %reduce-scatter.17.cloned.1.call-done = f32[16,1024]{1,0:T(8,128)} async-done(((f32[256,1024]{1,0:T(8,128)}), f32[16,1024]{1,0:T(8,128)}) %reduce-scatter.17.cloned.1.call-update) | async-done | bytes 65552 | tf_op jit(solution)/shard_map/reduce_scatter | solution.py:165
  599.5 5.0 collective-permute-start.1
  604.5 69.7 %reduce-scatter.19.cloned.1.call-done = f32[64,128]{1,0:T(8,128)} async-done(((f32[1024,128]{1,0:T(8,128)}), f32[64,128]{1,0:T(8,128)}) %reduce-scatter.19.cloned.1.call-update) | async-done | bytes 32784 | tf_op jit(solution)/shard_map/reduce_scatter | solution.py:165
  674.3 7.0 all-to-all-start.4
  683.5 2.6 all-to-all-done.4
  686.0 26.9 %reduce-scatter.15.cloned.1.call-done = f32[128,1024]{1,0:T(8,128)} async-done(((f32[1024,1024]{1,0:T(8,128)}), f32[128,1024]{1,0:T(8,128)}) %reduce-scatter.15.cloned.1.call-update) | async-done | bytes 524304 | tf_op jit(solution)/shard_map/reduce_scatter | solution.py:105
  714.3 68.7 %all-reduce = (f32[1024,8]{0,1:T(8,128)}, f32[1024]{0:T(1024)}, f32[1024]{0:T(1024)}, f32[512]{0:T(512)}, f32[1024]{0:T(1024)}) all-reduce(f32[1024,8]{0,1:T(8,128)S(1)} %fusion.102, f32[1024]{0:T(1024)S(1)} %get-tuple-element.17, f32[1024]{0:T(1024)S(1)} %dynamic_update_slice.6, ...), channel_id=1, replica_groups=mesh['seq'=16,'ctx'=8] {'seq','ctx'}, use_global_device_ids=true, to_apply=%region_28.29 | all-reduce | flops 11776 | bytes 94208 | tf_op jit(solution)/shard_map/psum | solution.py:172
  (228 shorter events, 41.9 us)
Async XLA Ops:
  8.0 165.6 %copy-start = (bf16[1024,8]{0,1:T(8,128)(2,1)S(1)}, bf16[1024,8]{0,1:T(8,128)(2,1)}, u32[]{:S(2)}) copy-start(bf16[1024,8]{0,1:T(8,128)(2,1)} %param.23) | copy-start | bytes 49156
  8.0 63.2 %all-gather.21.cloned.1.call-start = ((), (), s32[]{:S(2)}) async-start(), calls=%async_computation.27 | async-start | bytes 2359296 | tf_op jit(solution)/shard_map/all_gather | solution.py:65
  8.8 27.8 %all-to-all-start = ((bf16[8,8,128]{2,0,1:T(8,128)(2,1)}), bf16[8,8,128]{2,0,1:T(8,128)(2,1)S(1)}, u32[]{:S(2)}, u32[]{:S(2)}) async-start(bf16[8,8,128]{2,0,1:T(8,128)(2,1)} %bitcast.210), calls=%async_computation | async-start | bytes 32768 | tf_op jit(solution)/shard_map/all_to_all | solution.py:66
  15.6 130.4 %reduce-scatter.9.cloned.1.call-start = ((), (), s32[]{:S(2)}) async-start(), calls=%async_computation.15 | async-start | bytes 4718592 | tf_op jit(solution)/shard_map/reduce_scatter | solution.py:105
  15.6 38.2 %collective-permute-start = (bf16[16,1024]{1,0:T(8,128)(2,1)}, bf16[16,1024]{1,0:T(8,128)(2,1)S(1)}, u32[]{:S(2)}, u32[]{:S(2)}) collective-permute-start(bf16[16,1024]{1,0:T(8,128)(2,1)} %param.19), channel_id=1, source_target_pairs={{0,0},{8,1},{16,2},{24,3},{32,4},{40,5},{48,6},{56,7},{1,8},{9,9},... | collective-permute-start | bytes 98312 | tf_op jit(solution)/shard_map/ppermute | solution.py:67
  18.7 81.2 %copy-start.54 = (f32[32]{0:T(128)}, f32[32]{0:T(128)S(1)}, u32[]{:S(2)}) copy-start(f32[32]{0:T(128)S(1)} %multiply_power_fusion) | copy-start | bytes 388
  19.4 80.0 %copy-start.44 = (f32[128]{0:T(128)}, f32[128]{0:T(128)S(1)}, u32[]{:S(2)}) copy-start(f32[128]{0:T(128)S(1)} %dynamic-slice_convert_fusion) | copy-start | bytes 1540
  22.5 76.8 %copy-start.46 = (f32[64]{0:T(128)}, f32[64]{0:T(128)S(1)}, u32[]{:S(2)}) copy-start(f32[64]{0:T(128)S(1)} %dynamic-slice_convert_fusion.1) | copy-start | bytes 772
  23.2 52.7 %copy-start.31 = (f32[1024]{0:T(1024)}, f32[1024]{0:T(1024)S(1)}, u32[]{:S(2)}) copy-start(f32[1024]{0:T(1024)S(1)} %convert_element_type.74) | copy-start | bytes 12292
  36.5 63.4 %copy-start.34 = (f32[1,1024]{1,0:T(1,128)}, f32[1,1024]{1,0:T(1,128)S(1)}, u32[]{:S(2)}) copy-start(f32[1,1024]{1,0:T(1,128)S(1)} %convert_element_type.96) | copy-start | bytes 12292
  53.8 57.2 %copy-start.5 = (bf16[1024,128]{1,0:T(8,128)(2,1)}, bf16[1024,128]{1,0:T(8,128)(2,1)S(1)}, u32[]{:S(2)}) copy-start(bf16[1024,128]{1,0:T(8,128)(2,1)S(1)} %all_gather.44) | copy-start | bytes 786436
  111.0 11.6 %copy-start.52 = (bf16[1024]{0:T(1024)(128)(2,1)S(1)}, bf16[1024]{0:T(1024)(128)(2,1)}, u32[]{:S(2)}) copy-start(bf16[1024]{0:T(1024)(128)(2,1)} %param.27) | copy-start | bytes 6148
  111.0 35.0 %copy-start.3 = (bf16[1,128,1024]{2,1,0:T(8,128)(2,1)S(1)}, bf16[1,128,1024]{2,1,0:T(8,128)(2,1)}, u32[]{:S(2)}) copy-start(bf16[1,128,1024]{2,1,0:T(8,128)(2,1)} %param.15) | copy-start | bytes 786436
  113.8 34.9 %copy-start.30 = (bf16[8,8,512]{2,1,0:T(8,128)(2,1)S(1)}, bf16[8,8,512]{2,1,0:T(8,128)(2,1)}, u32[]{:S(2)}) copy-start(bf16[8,8,512]{2,1,0:T(8,128)(2,1)} %param.22) | copy-start | bytes 196612
  113.8 47.5 %copy-start.53 = (s32[1,128,4]{1,2,0:T(4,128)S(1)}, s32[1,128,4]{1,2,0:T(4,128)}, u32[]{:S(2)}) copy-start(s32[1,128,4]{1,2,0:T(4,128)} %param.18) | copy-start | bytes 6148
  113.9 60.9 %all-gather.15.cloned.1.call-start = ((), (), s32[]{:S(2)}) async-start(), calls=%async_computation.17 | async-start | bytes 2228224 | tf_op jit(solution)/shard_map/all_gather | solution.py:65
  122.5 69.6 %all-gather.13.cloned.1.call-start = ((), (), s32[]{:S(2)}) async-start(), calls=%async_computation.16 | async-start | bytes 2359296 | tf_op jit(solution)/shard_map/all_gather | solution.py:65
  122.6 26.1 %copy-start.24 = (f32[1024]{0:T(1024)}, f32[1024]{0:T(1024)S(1)}, u32[]{:S(2)}) copy-start(f32[1024]{0:T(1024)S(1)} %convert_element_type.83) | copy-start | bytes 12292
  147.8 44.3 %copy-start.42 = (f32[128]{0:T(128)}, f32[128]{0:T(128)S(1)}, u32[]{:S(2)}) copy-start(f32[128]{0:T(128)S(1)} %add_rsqrt_fusion.2) | copy-start | bytes 1540
  148.7 86.2 %all-gather.17.cloned.1.call-start = ((), (), s32[]{:S(2)}) async-start(), calls=%async_computation.18 | async-start | bytes 1114112 | tf_op jit(solution)/shard_map/all_gather | solution.py:65
  160.6 102.9 %all-gather.23.cloned.1.call-start = ((), (), s32[]{:S(2)}) async-start(), calls=%async_computation.28 | async-start | bytes 2359296 | tf_op jit(solution)/shard_map/all_gather | solution.py:65
  269.4 8.0 %all-to-all-start.3 = ((f32[8,128,1]{1,2,0:T(1,128)}), f32[8,128,1]{1,2,0:T(1,128)S(1)}, u32[]{:S(2)}, u32[]{:S(2)}) async-start(f32[8,128,1]{1,2,0:T(1,128)} %bitcast.31), calls=%async_computation.6 | async-start | bytes 8192 | tf_op jit(solution)/shard_map/all_to_all | solution.py:66
  272.8 63.5 %reduce-scatter.13.cloned.1.call-start = ((), (), s32[]{:S(2)}) async-start(), calls=%async_computation.20 | async-start | bytes 4718592 | tf_op jit(solution)/shard_map/reduce_scatter | solution.py:105
  301.9 66.2 %all-gather.19.cloned.1.call-start = ((), (), s32[]{:S(2)}) async-start(), calls=%async_computation.21 | async-start | bytes 2359296 | tf_op jit(solution)/shard_map/all_gather | solution.py:65
  340.3 103.4 %reduce-scatter.23.cloned.1.call-start = ((), (), s32[]{:S(2)}) async-start(), calls=%async_computation.26 | async-start | bytes 2228224 | tf_op jit(solution)/shard_map/reduce_scatter | solution.py:165
  345.1 179.2 %reduce-scatter.21.cloned.1.call-start = ((), (), s32[]{:S(2)}) async-start(), calls=%async_computation.25 | async-start | bytes 4456448 | tf_op jit(solution)/shard_map/reduce_scatter | solution.py:165
  351.6 16.5 %copy-start.6 = (bf16[1024,128]{1,0:T(8,128)(2,1)S(1)}, bf16[1024,128]{1,0:T(8,128)(2,1)}, u32[]{:S(2)}) copy-start(bf16[1024,128]{1,0:T(8,128)(2,1)} %copy-done.5) | copy-start | bytes 786436
  351.6 19.0 %copy-start.41 = (f32[2,1024]{1,0:T(2,128)S(1)}, f32[2,1024]{1,0:T(2,128)}, u32[]{:S(2)}) copy-start(f32[2,1024]{1,0:T(2,128)} %copy-done.40) | copy-start | bytes 24580
  351.6 247.8 %reduce-scatter.17.cloned.1.call-start = ((), (), s32[]{:S(2)}) async-start(), calls=%async_computation.23 | async-start | bytes 1114112 | tf_op jit(solution)/shard_map/reduce_scatter | solution.py:165
  404.8 269.4 %reduce-scatter.19.cloned.1.call-start = ((), (), s32[]{:S(2)}) async-start(), calls=%async_computation.24 | async-start | bytes 557056 | tf_op jit(solution)/shard_map/reduce_scatter | solution.py:165
  407.7 305.3 %reduce-scatter.15.cloned.1.call-start = ((), (), s32[]{:S(2)}) async-start(), calls=%async_computation.22 | async-start | bytes 4718592 | tf_op jit(solution)/shard_map/reduce_scatter | solution.py:105
  411.7 371.3 %reduce-scatter.11.cloned.1.call-start = ((), (), s32[]{:S(2)}) async-start(), calls=%async_computation.19 | async-start | bytes 4718592 | tf_op jit(solution)/shard_map/reduce_scatter | solution.py:105
  416.3 116.7 %copy-start.57 = (f32[128]{0:T(128)S(1)}, f32[128]{0:T(128)}, u32[]{:S(2)}) copy-start(f32[128]{0:T(128)} %get-tuple-element.40) | copy-start | bytes 1540
  416.3 265.0 %copy-start.4 = (bf16[128,1024]{1,0:T(8,128)(2,1)S(1)}, bf16[128,1024]{1,0:T(8,128)(2,1)}, u32[]{:S(2)}) copy-start(bf16[128,1024]{1,0:T(8,128)(2,1)} %multiply_convert_fusion.4) | copy-start | bytes 786436
  416.3 265.0 %copy-start.36 = (bf16[128,8]{0,1:T(8,128)(2,1)S(1)}, bf16[128,8]{0,1:T(8,128)(2,1)}, u32[]{:S(2)}) copy-start(bf16[128,8]{0,1:T(8,128)(2,1)} %multiply_convert_fusion.6) | copy-start | bytes 6148
  416.3 266.7 %copy-start.56 = (f32[128]{0:T(128)S(1)}, f32[128]{0:T(128)}, u32[]{:S(2)}) copy-start(f32[128]{0:T(128)} %get-tuple-element.11) | copy-start | bytes 1540
  416.3 266.9 %copy-start.58 = (f32[64]{0:T(128)S(1)}, f32[64]{0:T(128)}, u32[]{:S(2)}) copy-start(f32[64]{0:T(128)} %get-tuple-element.13) | copy-start | bytes 772
  416.3 296.6 %copy-start.33 = (f32[1024]{0:T(1024)S(1)}, f32[1024]{0:T(1024)}, u32[]{:S(2)}) copy-start(f32[1024]{0:T(1024)} %copy-done.31) | copy-start | bytes 12292
  416.4 297.9 %copy-start.37 = (f32[1024]{0:T(1024)S(1)}, f32[1024]{0:T(1024)}, u32[]{:S(2)}) copy-start(f32[1024]{0:T(1024)} %get-tuple-element.15) | copy-start | bytes 12292
  416.4 366.6 %copy-start.7 = (bf16[1,128,1024]{2,1,0:T(8,128)(2,1)S(1)}, bf16[1,128,1024]{2,1,0:T(8,128)(2,1)}, u32[]{:S(2)}) copy-start(bf16[1,128,1024]{2,1,0:T(8,128)(2,1)} %param.28) | copy-start | bytes 786436
  416.4 366.6 %copy-start.25 = (f32[1024]{0:T(1024)S(1)}, f32[1024]{0:T(1024)}, u32[]{:S(2)}) copy-start(f32[1024]{0:T(1024)} %copy-done.24) | copy-start | bytes 12292
  416.4 366.6 %copy-start.43 = (f32[128]{0:T(128)S(1)}, f32[128]{0:T(128)}, u32[]{:S(2)}) copy-start(f32[128]{0:T(128)} %copy-done.42) | copy-start | bytes 1540
  416.4 366.6 %copy-start.51 = (f32[128]{0:T(128)S(1)}, f32[128]{0:T(128)}, u32[]{:S(2)}) copy-start(f32[128]{0:T(128)} %copy-done.50) | copy-start | bytes 1540
  416.4 370.2 %copy-start.1 = (bf16[1024,8]{0,1:T(8,128)(2,1)S(1)}, bf16[1024,8]{0,1:T(8,128)(2,1)}, u32[]{:S(2)}) copy-start(bf16[1024,8]{0,1:T(8,128)(2,1)} %param.23) | copy-start | bytes 49156
  445.4 80.7 %all-to-all-start.6 = ((f32[64,1,512]{2,1,0:T(1,128)}), f32[64,1,512]{2,1,0:T(1,128)S(1)}, u32[]{:S(2)}, u32[]{:S(2)}) async-start(f32[64,1,512]{2,1,0:T(1,128)} %copy.68), calls=%async_computation.14 | async-start | bytes 262144 | tf_op jit(solution)/shard_map/all_to_all | solution.py:66
  526.2 78.4 %all-to-all-start.5 = ((f32[64,1,1024]{2,1,0:T(1,128)}), f32[64,1,1024]{2,1,0:T(1,128)S(1)}, u32[]{:S(2)}, u32[]{:S(2)}) async-start(f32[64,1,1024]{2,1,0:T(1,128)} %copy.66), calls=%async_computation.12 | async-start | bytes 524288 | tf_op jit(solution)/shard_map/all_to_all | solution.py:66
  599.5 86.5 %collective-permute-start.1 = (f32[16,1024]{1,0:T(8,128)}, f32[16,1024]{1,0:T(8,128)S(1)}, u32[]{:S(2)}, u32[]{:S(2)}) collective-permute-start(f32[16,1024]{1,0:T(8,128)} %reduce-scatter.17.cloned.1.call-done), channel_id=1, source_target_pairs={{0,0},{1,8},{2,16},{3,24},{4,32},{5,40},{6,48},{7,56},{8,1},{9,9},... | collective-permute-start | bytes 196616 | tf_op jit(solution)/shard_map/ppermute | solution.py:166
  674.3 11.7 %all-to-all-start.4 = ((f32[8,8,128]{2,1,0:T(8,128)}), f32[8,8,128]{2,1,0:T(8,128)S(1)}, u32[]{:S(2)}, u32[]{:S(2)}) async-start(f32[8,8,128]{2,1,0:T(8,128)} %bitcast.200), calls=%async_computation.10 | async-start | bytes 65536 | tf_op jit(solution)/shard_map/all_to_all | solution.py:66
  (37 other events, 127.9 us)
Sparse Core Ops, SparseCore 0:
  10.6 28.9 all-gather.20
  114.0 31.9 reduce-scatter.8
  302.0 34.3 reduce-scatter.12
Sparse Core Ops, SparseCore 1:
  122.6 40.5 all-gather.14
  165.3 26.8 all-gather.12
  194.2 40.6 all-gather.16
  236.6 26.9 all-gather.22
  340.4 27.7 all-gather.18
  371.4 72.2 reduce-scatter.22
  447.3 76.9 reduce-scatter.20
  527.3 72.1 reduce-scatter.16
  602.9 71.3 reduce-scatter.18
  676.7 36.2 reduce-scatter.14
  715.2 37.0 reduce-scatter.10
